TPU v7x, 32 devices: a whole 2x2x4 slice. The times are simulated.
32 devices in a mesh: dp: 16 (over z, y, x), tile: 2 (over core).
Axes of the slice: x: 2, y: 2, z: 4, core: 2. Of those that a mesh axis runs over, the one named last changes fastest.
Arguments:
- snapshots: bfloat16 [8208, 3, 32, 128], P('dp', None, 'tile'), may hold values from -16 to 16, as said below
- pair_start: int32 [8192], P('dp'), may hold values from 0 to 511
- bath_class: int32 [32, 128], P('tile'), may hold values from 0 to 3
- stencil_w: float32 [3, 3, 3, 9], replicated, may hold values from -1.25 to 1.25
- depth_gain: float32 [3, 4], replicated, may hold values from 0.5 to 2
- stencil_bias: float32 [3, 3], replicated, may hold values from -2 to 2
- readout: float32 [3], replicated, may hold values from -3.5 to 3.5
- panel_order: int32 [8], replicated, may hold values from 0 to 7, each once
Outputs:
- chol_panels: float32 [2, 2048, 1024], P('tile', 'dp')
- cross_whitened: float32 [2, 2048, 1024], P('tile', 'dp')
- ridge_shift: float32 [], replicated
Inputs may be any that keep to these rules, and one draw needn't show every extreme that they name: snapshots stay within the range. The pair's second snapshot is the next one, pair_start + 1, of the same index of dp. `panel_order`: each block number appears once.
All inputs are finite; a program needn't handle non-finite values.
Results may differ from a plain program's by a relative error of at most 0.0032.
Values may be sent and summed in bfloat16 or wider, within the bound.
No kernel may reach another device: no remote copies, remote signals or barrier semaphores. Data moves between devices by JAX's collectives and lax.ppermute only.
A program may use at most 192 MiB of HBM per device.

v0:
```python
import jax
import jax.numpy as jnp
from jax import lax
from jax.sharding import PartitionSpec as P

PANEL = 512
ridge_factor = 0.5


def extended(block, sides, width):
    for axis, dim in sides:
        count = lax.axis_size(axis)
        forward = [(i, i + 1) for i in range(count - 1)]
        backward = [(target, source) for source, target in forward]
        low = lax.ppermute(
            lax.slice_in_dim(block, block.shape[dim] - width, None, axis=dim), axis, forward
        )
        high = lax.ppermute(lax.slice_in_dim(block, 0, width, axis=dim), axis, backward)
        block = jnp.concatenate([low, block, high], axis=dim)
    return block


def gain_field(classes, gains):
    field = jnp.zeros(classes.shape, jnp.float32)
    for class_idx in range(gains.shape[0]):
        field = field + jnp.where(
            classes == class_idx, gains[class_idx], jnp.zeros((), jnp.float32)
        )
    return field


def layer_step(padded_rows, gains_map, weights, bias):
    fields_count = padded_rows.shape[1]
    kernel = weights.reshape(fields_count, fields_count, 3, 3)
    stencil_sum = lax.conv_general_dilated(
        padded_rows,
        kernel,
        (1, 1),
        ((0, 0), (1, 1)),
        dimension_numbers=("NCHW", "OIHW", "NCHW"),
        precision=lax.Precision.HIGHEST,
        preferred_element_type=jnp.float32,
    )
    centre = padded_rows[:, :, 1:-1, :]
    return centre + jnp.tanh(gains_map[None, None] * stencil_sum + bias[None, :, None, None])


def readout_sum(fields, readout):
    result = jnp.zeros((fields.shape[0], fields.shape[2], fields.shape[3]), jnp.float32)
    for field_idx in range(fields.shape[1]):
        result = result + readout[field_idx] * fields[:, field_idx]
    return result


def right_solve(lower_factor, rows_in):
    return lax.linalg.triangular_solve(
        lower_factor, rows_in, left_side=False, lower=True, transpose_a=True
    )


def panel_factor(diag_rows):
    lead = jnp.linalg.cholesky(diag_rows[:PANEL, :PANEL])
    below = right_solve(lead, diag_rows[PANEL:, :PANEL])
    rest = diag_rows[PANEL:, PANEL:] - jnp.dot(below, below.T, precision=lax.Precision.HIGHEST)
    tail = jnp.linalg.cholesky(rest)
    return (lead, below, tail)


def apply_factor(rows_in, lead, below, tail):
    left = right_solve(lead, rows_in[:, :PANEL])
    inner = rows_in[:, PANEL:] - jnp.dot(left, below.T, precision=lax.Precision.HIGHEST)
    right = right_solve(tail, inner)
    return jnp.concatenate([left, right], axis=1)


def contract(source, panel, row_count):
    part_cols = lax.slice_in_dim(source, 0, row_count, axis=1)
    return lax.dot_general(
        part_cols, panel, (((0,), (0,)), ((), ())), preferred_element_type=jnp.float32
    )


def on_device(
    snapshots, pair_start, bath_class, stencil_w, depth_gain, stencil_bias, readout, panel_order
):
    tile_pos = lax.axis_index("tile")
    dp_pos = lax.axis_index("dp")
    tile_count = lax.axis_size("tile")
    dp_count = lax.axis_size("dp")
    layer_count = stencil_w.shape[0]
    tile_rows = bath_class.shape[0]
    grid_cols = bath_class.shape[1]
    tile_obs = tile_rows * grid_cols
    own_rows = tile_obs // dp_count
    width = 2 * PANEL
    snap_count = snapshots.shape[0]
    fields = snapshots.astype(jnp.float32)
    for layer_idx in range(layer_count):
        padded = extended(fields, (("tile", 2),), 1)
        gains_map = gain_field(bath_class, depth_gain[layer_idx])
        fields = layer_step(padded, gains_map, stencil_w[layer_idx], stencil_bias[layer_idx])
    encoded = readout_sum(fields, readout).reshape(snap_count, tile_obs).astype(jnp.bfloat16)
    earlier = jnp.take(encoded, pair_start, axis=0)
    later = jnp.take(encoded, pair_start + 1, axis=0)
    first_block = panel_order[0]
    second_block = panel_order[1]
    every_col = lax.all_gather(earlier, "tile", axis=1, tiled=True)
    panel = jnp.concatenate(
        [
            lax.dynamic_slice_in_dim(every_col, first_block * PANEL, PANEL, 1),
            lax.dynamic_slice_in_dim(every_col, second_block * PANEL, PANEL, 1),
        ],
        axis=1,
    )
    energy_sum = lax.psum(jnp.sum(jnp.square(earlier.astype(jnp.float32))), ("dp", "tile"))
    pairs_total = float(pair_start.shape[0] * dp_count)
    shift_value = ridge_factor * (energy_sum / pairs_total) / float(tile_obs * tile_count)
    grow_start = tile_pos * tile_obs + dp_pos * own_rows
    own_block = grow_start // PANEL
    offset = grow_start - own_block * PANEL
    gram_own = (
        lax.psum_scatter(
            contract(earlier, panel, lax.axis_size("dp") * own_rows),
            "dp",
            scatter_dimension=0,
            tiled=True,
        )
        / pairs_total
    )
    placed = lax.dynamic_update_slice_in_dim(
        jnp.zeros((PANEL, width), jnp.float32), gram_own, offset, 0
    )
    diag_part = jnp.concatenate(
        [
            jnp.where(own_block == first_block, placed, 0.0),
            jnp.where(own_block == second_block, placed, 0.0),
        ],
        axis=0,
    )
    diag_rows = lax.psum(diag_part, ("dp", "tile"))
    cross_own = (
        lax.psum_scatter(
            contract(later, panel, lax.axis_size("dp") * own_rows),
            "dp",
            scatter_dimension=0,
            tiled=True,
        )
        / pairs_total
    )
    diag_rows = diag_rows + shift_value * jnp.eye(width, dtype=jnp.float32)
    row_obs = grow_start + jnp.arange(own_rows, dtype=jnp.int32)[:, None]
    col_obs = jnp.concatenate(
        [
            first_block * PANEL + jnp.arange(PANEL, dtype=jnp.int32),
            second_block * PANEL + jnp.arange(PANEL, dtype=jnp.int32),
        ]
    )[None, :]
    shifted = gram_own + shift_value * (row_obs == col_obs).astype(jnp.float32)
    lead, below, tail = panel_factor(diag_rows)
    computed = apply_factor(shifted, lead, below, tail)
    panel_full = jnp.concatenate(
        [
            jnp.concatenate([lead, jnp.zeros_like(lead)], axis=1),
            jnp.concatenate([below, tail], axis=1),
        ],
        axis=0,
    )
    first_piece = lax.dynamic_slice_in_dim(panel_full, offset, own_rows, 0)
    second_piece = lax.dynamic_slice_in_dim(panel_full, PANEL + offset, own_rows, 0)
    factor_rows = jnp.where(
        own_block == first_block,
        first_piece,
        jnp.where(own_block == second_block, second_piece, computed),
    )
    whitened = apply_factor(cross_own, lead, below, tail)
    return (factor_rows[None], whitened[None], shift_value)


def solution(mesh):
    placed = (P("dp", None, "tile", None), P("dp"), P("tile", None), P(), P(), P(), P(), P())
    return jax.shard_map(
        on_device,
        mesh=mesh,
        in_specs=placed,
        out_specs=(P("tile", "dp", None), P("tile", "dp", None), P()),
        check_vma=False,
    )
```

profile of v0, /device:TPU:0, one launch (start us, length us, event | category | flops | bytes accessed | tf_op | source)
XLA Modules:
  0.0 1661.3 jit_solution(145919323454137758)
XLA Ops:
  7.2 3.9 fusion.152
  16.2 8.4 convert_element_type.14
  29.0 5.6 select_add_fusion.3
  34.6 12.8 pad_maximum_fusion
  47.5 21.0 %copy.141 = f32[513,3,18,128]{0,1,3,2:T(4,128)} copy(f32[513,3,18,128]{3,2,1,0:T(8,128)} %pad_maximum_fusion) | data formatting | bytes 28366848 | tf_op jit(solution)/shard_map/concatenate | solution.py:19
  68.5 171.2 %fusion.157 = f32[513,3,16,128]{0,1,3,2:T(4,128)} fusion(f32[513,3,18,128]{0,1,3,2:T(4,128)} %copy.141, f32[3,3,3,3]{1,0,3,2:T(4,128)S(1)} %bitcast.202), kind=kOutput, calls=%fused_computation.288 | convolution fusion | flops 1015887744 | bytes 26791236 | tf_op jit(solution)/shard_map/conv_general_dilated | solution.py:35
  239.6 16.2 copy.143
  255.9 7.9 tanh_add_fusion.2
  263.8 4.5 copy-done.1
  276.6 12.8 pad_maximum_fusion.1
  289.5 21.0 %copy.144 = f32[513,3,18,128]{0,1,3,2:T(4,128)} copy(f32[513,3,18,128]{3,2,1,0:T(8,128)} %pad_maximum_fusion.1) | data formatting | bytes 28366848 | tf_op jit(solution)/shard_map/concatenate | solution.py:19
  310.4 170.7 %fusion.158 = f32[513,3,16,128]{0,1,3,2:T(4,128)} fusion(f32[513,3,18,128]{0,1,3,2:T(4,128)} %copy.144, f32[3,3,3,3]{1,0,3,2:T(4,128)S(1)} %bitcast.204), kind=kOutput, calls=%fused_computation.289 | convolution fusion | flops 1015887744 | bytes 26791236 | tf_op jit(solution)/shard_map/conv_general_dilated | solution.py:35
  481.1 16.3 copy.146
  497.4 9.7 tanh_add_fusion.1
  507.1 4.5 copy-done
  518.9 12.8 pad_maximum_fusion.2
  531.8 21.0 %copy.147 = f32[513,3,18,128]{0,1,3,2:T(4,128)} copy(f32[513,3,18,128]{3,2,1,0:T(8,128)} %pad_maximum_fusion.2) | data formatting | bytes 28366848 | tf_op jit(solution)/shard_map/concatenate | solution.py:19
  552.7 170.7 %fusion.159 = f32[513,3,16,128]{0,1,3,2:T(4,128)} fusion(f32[513,3,18,128]{0,1,3,2:T(4,128)} %copy.147, f32[3,3,3,3]{1,0,3,2:T(4,128)S(1)} %bitcast.203), kind=kOutput, calls=%fused_computation.290 | convolution fusion | flops 1015887744 | bytes 26791236 | tf_op jit(solution)/shard_map/conv_general_dilated | solution.py:35
  723.4 16.3 copy.149
  739.6 9.4 tanh_add_fusion
  752.8 3.3 gather_fusion
  756.1 4.0 multiply_reduce_fusion
  762.1 14.0 all-gather.2.cloned.1.call-done
  777.3 7.2 fusion.18
  784.6 3.3 gather_fusion.1
  787.9 7.3 fusion.4
  796.6 45.6 %psum.15 = f32[]{:T(128)} all-reduce(f32[]{:T(128)} %get-tuple-element.74), channel_id=1, replica_groups=mesh['dp'=16,'tile'=2] {'dp','tile'}, use_global_device_ids=true, to_apply=%region_3.5 | all-reduce | flops 1 | bytes 8 | tf_op jit(solution)/shard_map/psum | solution.py:115
  842.9 122.0 %reduce-scatter.3.cloned.1.call-done = f32[128,1024]{0,1:T(8,128)} async-done(((f32[2048,1024]{0,1:T(8,128)}), f32[128,1024]{0,1:T(8,128)}) %reduce-scatter.3.cloned.1.call-update) | async-done | bytes 524304 | tf_op jit(solution)/shard_map/reduce_scatter | solution.py:122
  970.1 178.3 %reduce-scatter.5.cloned.1.call-done = f32[128,1024]{0,1:T(8,128)} async-done(((f32[2048,1024]{0,1:T(8,128)}), f32[128,1024]{0,1:T(8,128)}) %reduce-scatter.5.cloned.1.call-update) | async-done | bytes 524304 | tf_op jit(solution)/shard_map/reduce_scatter | solution.py:142
  1150.3 147.7 %all-reduce.4.cloned.1.call-done = f32[1024,1024]{0,1:T(8,128)} async-done(((f32[1024,1024]{0,1:T(8,128)}), f32[1024,1024]{0,1:T(8,128)}) %all-reduce.4.cloned.1.call-update) | async-done | bytes 4194320 | tf_op jit(solution)/shard_map/psum | solution.py:140
  1304.4 11.7 cholesky.286
  1316.3 9.8 custom-call.33
  1326.7 12.2 cholesky.305
  1340.3 9.8 custom-call.34
  1350.7 11.7 cholesky.326
  1363.2 9.8 custom-call.35
  1373.6 11.8 cholesky.343
  1389.9 7.8 while.9
  1397.7 39.3 %custom-call.26 = f32[4,128,128]{1,2,0:T(8,128)S(1)} custom-call(f32[4,128,128]{2,1,0:T(8,128)S(1)} %get-tuple-element.21), custom_call_target="InvertDiagBlocksLowerTriangular" | custom-call | tf_op jit(solution)/shard_map/triangular_solve | solution.py:56
  1450.8 11.7 cholesky.358
  1463.2 9.8 custom-call.36
  1485.7 12.3 cholesky.377
  1501.3 10.4 custom-call.37
  1514.8 12.3 cholesky.398
  1528.7 10.6 custom-call.38
  1541.6 12.3 cholesky.415
  1567.1 13.7 while.10
  1580.8 41.0 %custom-call.40 = f32[4,128,128]{1,2,0:T(8,128)} custom-call(f32[4,128,128]{2,1,0:T(8,128)} %get-tuple-element.41), custom_call_target="InvertDiagBlocksLowerTriangular" | custom-call | tf_op jit(solution)/shard_map/triangular_solve/custom-call.8 | solution.py:56
  (225 shorter events, 151.0 us)
Async XLA Ops:
  7.2 768.9 %all-gather.2.cloned.1.call-start = ((), (), s32[]{:S(2)}) async-start(), calls=%async_computation.2 | async-start | bytes 6291456 | tf_op jit(solution)/shard_map/all_gather | solution.py:107
  11.1 23.5 %collective-permute-start = (f32[513,3,1,128]{3,2,1,0:T(1,128)S(1)}, f32[513,3,1,128]{3,2,1,0:T(1,128)S(1)}, u32[]{:S(2)}, u32[]{:S(2)}) collective-permute-start(f32[513,3,1,128]{3,2,1,0:T(1,128)S(1)} %get-tuple-element.89), channel_id=1, source_target_pairs={{0,1},{2,3},{4,5},{6,7},{8,9},{10,11},{12,13},{14,15},{16,17},{18,... | collective-permute-start | bytes 2363912 | tf_op jit(solution)/shard_map/ppermute | solution.py:15
  13.6 21.1 %collective-permute-start.1 = (f32[513,3,1,128]{3,2,1,0:T(1,128)S(1)}, f32[513,3,1,128]{3,2,1,0:T(1,128)S(1)}, u32[]{:S(2)}, u32[]{:S(2)}) collective-permute-start(f32[513,3,1,128]{3,2,1,0:T(1,128)S(1)} %get-tuple-element.90), channel_id=1, source_target_pairs={{1,0},{3,2},{5,4},{7,6},{9,8},{11,10},{13,12},{15,14},{17,16},{19,... | collective-permute-start | bytes 2363912 | tf_op jit(solution)/shard_map/ppermute | solution.py:18
  16.2 8.5 copy-start.19
  16.2 9.2 copy-start.26
  16.2 9.7 copy-start.21
  263.8 4.5 copy-start.1
  269.3 5.0 collective-permute-start.2
  272.5 4.2 collective-permute-start.3
  481.1 16.3 copy-start.16
  481.1 16.3 copy-start.24
  497.4 18.7 %copy-start.18 = (f32[1,3,3,9]{3,2,1,0:T(4,128)S(1)}, f32[1,3,3,9]{3,2,1,0:T(4,128)}, u32[]{:S(2)}) copy-start(f32[1,3,3,9]{3,2,1,0:T(4,128)} %get-tuple-element.119) | copy-start | bytes 976
  497.4 18.8 %copy-start.20 = (s32[512]{0:T(512)S(1)}, s32[512]{0:T(512)}, u32[]{:S(2)}) copy-start(s32[512]{0:T(512)} %param.14) | copy-start | bytes 6148
  497.4 18.8 %copy-start.22 = (f32[3]{0:T(128)S(1)}, f32[3]{0:T(128)}, u32[]{:S(2)}) copy-start(f32[3]{0:T(128)} %param.19) | copy-start | bytes 40
  507.1 4.5 copy-start
  512.6 4.2 collective-permute-start.4
  514.7 4.2 collective-permute-start.5
  723.4 16.3 copy-start.17
  723.4 16.3 copy-start.23
  756.1 4.1 copy-start.25
  760.1 204.7 %reduce-scatter.3.cloned.1.call-start = ((), (), s32[]{:S(2)}) async-start(), calls=%async_computation.3 | async-start | bytes 8912896 | tf_op jit(solution)/shard_map/reduce_scatter | solution.py:122
  784.6 363.8 %reduce-scatter.5.cloned.1.call-start = ((), (), s32[]{:S(2)}) async-start(), calls=%async_computation.5 | async-start | bytes 8912896 | tf_op jit(solution)/shard_map/reduce_scatter | solution.py:142
  795.2 502.8 %all-reduce.4.cloned.1.call-start = ((), (), s32[]{:S(2)}) async-start(), calls=%async_computation.4 | async-start | bytes 8388608 | tf_op jit(solution)/shard_map/psum | solution.py:140
  1300.5 1.9 copy-start.2
  1449.8 1.0 copy-start.5
  1462.6 0.6 copy-start.14
  1514.2 0.7 copy-start.11
  1580.8 49.8 %copy-start.3 = (f32[512,512]{1,0:T(8,128)S(1)}, f32[512,512]{1,0:T(8,128)}, u32[]{:S(2)}) copy-start(f32[512,512]{1,0:T(8,128)} %get-tuple-element.253) | copy-start | bytes 3145732
  1624.4 1.6 copy-start.9
  1626.0 2.8 copy-start.12
  1628.8 1.2 copy-start.15
  1630.0 0.6 copy-start.8
  1633.0 8.2 copy-start.6
  1638.2 12.1 copy-start.4
  1646.6 5.8 copy-start.7
  1646.7 5.8 copy-start.10
  1646.7 5.8 copy-start.13
Sparse Core Ops, SparseCore 0:
  760.3 15.7 all-gather.1
  784.7 180.1 reduce-scatter.2
  967.2 181.1 reduce-scatter.4
  1153.8 144.1 all-reduce.3
where the time goes:
time: 1670 us; the launch traced here: 1660 us
  matrix products  575 us (34%)
  waiting for transfers between devices  467 us (28%)
  other arithmetic  353 us (21%)
  local copies, waits for them, and re-layouts  186 us (11%)
  blocking collectives  45.6 us (3%)
  between operations  24.3 us (1%)
    conv_general_dilated x3, matrix products, layer_step(): lax.conv_general_dilated(padded_rows, kernel, (1, 1), ((0, 0), (1, 1)), d...  512 us
    reduce_scatter x1, waiting for transfers between devices, on_device(): lax.psum_scatter(contract(later, panel, lax.axis_size('dp') * own_rows),...  178 us
    psum x1, waiting for transfers between devices, on_device(): diag_rows = lax.psum(diag_part, ('dp', 'tile'))  148 us
    reduce_scatter x1, waiting for transfers between devices, on_device(): lax.psum_scatter(contract(earlier, panel, lax.axis_size('dp') * own_rows)...  122 us
    another operation x15, other arithmetic, panel_factor(): tail = jnp.linalg.cholesky(rest)  84.9 us
    another operation x4, other arithmetic, right_solve(): lax.linalg.triangular_solve(lower_factor, rows_in, left_side=False, lower...  81.6 us
    another operation x15, other arithmetic, panel_factor(): lead = jnp.linalg.cholesky(diag_rows[:PANEL, :PANEL])  79.7 us
    concatenate x3, local copies, waits for them, and re-layouts, extended(): block = jnp.concatenate([low, block, high], axis=dim)  62.9 us
  transfers between devices with their start and end apart: 10, of which 7 were waited for; matrix products, arithmetic and copies ran while one was open for 2% of the time, Pallas kernels for 0%

commit v1 on v0

--- a/solution.py
+++ b/solution.py
@@ -137,7 +137,7 @@
         ],
         axis=0,
     )
-    diag_rows = lax.psum(diag_part, ("dp", "tile"))
+    diag_rows = lax.psum(lax.psum(diag_part, "tile"), "dp")
     cross_own = (
         lax.psum_scatter(
             contract(later, panel, lax.axis_size("dp") * own_rows),

time: 1670 us -> 1740 us (1.042)
  waiting for transfers between devices: 467 us -> 520 us
    psum x1 -> x2, waiting for transfers between devices: 148 us -> 194 us  [on_device(): diag_rows = lax.psum(lax.psum(diag_part, 'tile'), 'dp')]
  transfers between devices with their start and end apart: 10 -> 11, of which waited for: 7 -> 8; matrix products, arithmetic and copies ran while one was open for 2% -> 2% of each run, Pallas kernels for 0% -> 0%
where the time goes in v1:
time: 1740 us; the launch traced here: 1730 us
  matrix products  576 us (33%)
  waiting for transfers between devices  520 us (30%)
  other arithmetic  363 us (21%)
  local copies, waits for them, and re-layouts  185 us (11%)
  blocking collectives  52.1 us (3%)
  between operations  24.4 us (1%)
    conv_general_dilated x3, matrix products, layer_step(): lax.conv_general_dilated(padded_rows, kernel, (1, 1), ((0, 0), (1, 1)), d...  512 us
    psum x2, waiting for transfers between devices, on_device(): diag_rows = lax.psum(lax.psum(diag_part, 'tile'), 'dp')  194 us
    reduce_scatter x1, waiting for transfers between devices, on_device(): lax.psum_scatter(contract(later, panel, lax.axis_size('dp') * own_rows),...  181 us
    reduce_scatter x1, waiting for transfers between devices, on_device(): lax.psum_scatter(contract(earlier, panel, lax.axis_size('dp') * own_rows)...  126 us
    another operation x15, other arithmetic, panel_factor(): tail = jnp.linalg.cholesky(rest)  84.9 us
    another operation x4, other arithmetic, right_solve(): lax.linalg.triangular_solve(lower_factor, rows_in, left_side=False, lower...  81.6 us
    another operation x15, other arithmetic, panel_factor(): lead = jnp.linalg.cholesky(diag_rows[:PANEL, :PANEL])  79.6 us
    concatenate x3, local copies, waits for them, and re-layouts, extended(): block = jnp.concatenate([low, block, high], axis=dim)  62.9 us
  transfers between devices with their start and end apart: 11, of which 8 were waited for; matrix products, arithmetic and copies ran while one was open for 2% of the time, Pallas kernels for 0%

profile of v1, /device:TPU:0, one launch (start us, length us, event | category | flops | bytes accessed | tf_op | source)
XLA Modules:
  0.0 1732.4 jit_solution(13702099503364767665)
XLA Ops:
  7.2 3.9 fusion.152
  16.2 8.4 convert_element_type.14
  29.0 5.6 select_add_fusion.3
  34.6 12.8 pad_maximum_fusion
  47.5 21.0 %copy.141 = f32[513,3,18,128]{0,1,3,2:T(4,128)} copy(f32[513,3,18,128]{3,2,1,0:T(8,128)} %pad_maximum_fusion) | data formatting | bytes 28366848 | tf_op jit(solution)/shard_map/concatenate | solution.py:19
  68.5 171.0 %fusion.157 = f32[513,3,16,128]{0,1,3,2:T(4,128)} fusion(f32[513,3,18,128]{0,1,3,2:T(4,128)} %copy.141, f32[3,3,3,3]{1,0,3,2:T(4,128)S(1)} %bitcast.202), kind=kOutput, calls=%fused_computation.288 | convolution fusion | flops 1015887744 | bytes 26791236 | tf_op jit(solution)/shard_map/conv_general_dilated | solution.py:35
  239.5 16.2 copy.143
  255.7 18.2 %tanh_add_fusion.2 = f32[513,3,16,128]{3,2,1,0:T(8,128)S(1)} fusion(f32[513,3,16,128]{3,2,1,0:T(8,128)} %copy.143, f32[3]{0:T(128)S(1)} %get-tuple-element.129, f32[16,128]{1,0:T(8,128)S(1)} %get-tuple-element.123, bf16[513,3,16,128]{3,2,1,0:T(8,128)(2,1)} %param.13), kind=kLoop, calls=%fused_computation.11 | loop fusion | flops 12607488 | bytes 31526924 | tf_op jit(solution)/shard_map/add | solution.py:45
  274.0 4.5 copy-done.1
  286.9 12.8 pad_maximum_fusion.1
  299.7 21.0 %copy.144 = f32[513,3,18,128]{0,1,3,2:T(4,128)} copy(f32[513,3,18,128]{3,2,1,0:T(8,128)} %pad_maximum_fusion.1) | data formatting | bytes 28366848 | tf_op jit(solution)/shard_map/concatenate | solution.py:19
  320.7 170.7 %fusion.158 = f32[513,3,16,128]{0,1,3,2:T(4,128)} fusion(f32[513,3,18,128]{0,1,3,2:T(4,128)} %copy.144, f32[3,3,3,3]{1,0,3,2:T(4,128)S(1)} %bitcast.204), kind=kOutput, calls=%fused_computation.289 | convolution fusion | flops 1015887744 | bytes 26791236 | tf_op jit(solution)/shard_map/conv_general_dilated | solution.py:35
  491.3 16.3 copy.146
  507.6 9.7 tanh_add_fusion.1
  517.3 4.5 copy-done
  529.1 12.8 pad_maximum_fusion.2
  542.0 21.0 %copy.147 = f32[513,3,18,128]{0,1,3,2:T(4,128)} copy(f32[513,3,18,128]{3,2,1,0:T(8,128)} %pad_maximum_fusion.2) | data formatting | bytes 28366848 | tf_op jit(solution)/shard_map/concatenate | solution.py:19
  562.9 170.7 %fusion.159 = f32[513,3,16,128]{0,1,3,2:T(4,128)} fusion(f32[513,3,18,128]{0,1,3,2:T(4,128)} %copy.147, f32[3,3,3,3]{1,0,3,2:T(4,128)S(1)} %bitcast.203), kind=kOutput, calls=%fused_computation.290 | convolution fusion | flops 1015887744 | bytes 26791236 | tf_op jit(solution)/shard_map/conv_general_dilated | solution.py:35
  733.6 16.3 copy.149
  749.9 9.4 tanh_add_fusion
  766.3 4.0 multiply_reduce_fusion
  772.3 14.0 all-gather.2.cloned.1.call-done
  787.5 7.2 fusion.18
  796.2 52.1 %psum.23 = f32[]{:T(128)} all-reduce(f32[]{:T(128)} %get-tuple-element.74), channel_id=1, replica_groups=mesh['dp'=16,'tile'=2] {'dp','tile'}, use_global_device_ids=true, to_apply=%region_4.6 | all-reduce | flops 1 | bytes 8 | tf_op jit(solution)/shard_map/psum | solution.py:115
  849.0 125.9 %reduce-scatter.3.cloned.1.call-done = f32[128,1024]{0,1:T(8,128)} async-done(((f32[2048,1024]{0,1:T(8,128)}), f32[128,1024]{0,1:T(8,128)}) %reduce-scatter.3.cloned.1.call-update) | async-done | bytes 524304 | tf_op jit(solution)/shard_map/reduce_scatter | solution.py:122
  980.2 3.3 gather_fusion.1
  983.5 8.5 fusion.4
  992.4 18.6 %all-reduce.5.cloned.1.call-done = f32[1024,1024]{0,1:T(8,128)} async-done(((f32[1024,1024]{0,1:T(8,128)}), f32[1024,1024]{0,1:T(8,128)}) %all-reduce.5.cloned.1.call-update) | async-done | bytes 4194320 | tf_op jit(solution)/shard_map/psum | solution.py:140
  1011.0 181.2 %reduce-scatter.5.cloned.1.call-done = f32[128,1024]{0,1:T(8,128)} async-done(((f32[2048,1024]{0,1:T(8,128)}), f32[128,1024]{0,1:T(8,128)}) %reduce-scatter.5.cloned.1.call-update) | async-done | bytes 524304 | tf_op jit(solution)/shard_map/reduce_scatter | solution.py:142
  1194.1 175.2 %all-reduce.7.cloned.1.call-done = f32[1024,1024]{0,1:T(8,128)} async-done(((f32[1024,1024]{0,1:T(8,128)}), f32[1024,1024]{0,1:T(8,128)}) %all-reduce.7.cloned.1.call-update) | async-done | bytes 4194320 | tf_op jit(solution)/shard_map/psum | solution.py:140
  1375.7 11.7 cholesky.286
  1387.6 9.8 custom-call.33
  1398.1 11.7 cholesky.305
  1411.1 10.0 custom-call.34
  1421.8 11.7 cholesky.326
  1434.2 9.8 custom-call.35
  1444.7 12.1 cholesky.343
  1461.2 7.8 while.9
  1469.0 39.3 %custom-call.26 = f32[4,128,128]{1,2,0:T(8,128)S(1)} custom-call(f32[4,128,128]{2,1,0:T(8,128)S(1)} %get-tuple-element.21), custom_call_target="InvertDiagBlocksLowerTriangular" | custom-call | tf_op jit(solution)/shard_map/triangular_solve | solution.py:56
  1522.1 11.7 cholesky.358
  1534.5 9.8 custom-call.36
  1556.8 12.3 cholesky.377
  1572.3 10.4 custom-call.37
  1585.9 12.3 cholesky.398
  1599.7 10.6 custom-call.38
  1612.7 12.3 cholesky.415
  1638.2 13.7 while.10
  1651.9 41.1 %custom-call.40 = f32[4,128,128]{1,2,0:T(8,128)} custom-call(f32[4,128,128]{2,1,0:T(8,128)} %get-tuple-element.41), custom_call_target="InvertDiagBlocksLowerTriangular" | custom-call | tf_op jit(solution)/shard_map/triangular_solve/custom-call.8 | solution.py:56
  (228 shorter events, 154.6 us)
Async XLA Ops:
  7.2 779.1 %all-gather.2.cloned.1.call-start = ((), (), s32[]{:S(2)}) async-start(), calls=%async_computation.2 | async-start | bytes 6291456 | tf_op jit(solution)/shard_map/all_gather | solution.py:107
  11.1 23.5 %collective-permute-start = (f32[513,3,1,128]{3,2,1,0:T(1,128)S(1)}, f32[513,3,1,128]{3,2,1,0:T(1,128)S(1)}, u32[]{:S(2)}, u32[]{:S(2)}) collective-permute-start(f32[513,3,1,128]{3,2,1,0:T(1,128)S(1)} %get-tuple-element.89), channel_id=1, source_target_pairs={{0,1},{2,3},{4,5},{6,7},{8,9},{10,11},{12,13},{14,15},{16,17},{18,... | collective-permute-start | bytes 2363912 | tf_op jit(solution)/shard_map/ppermute | solution.py:15
  13.6 21.1 %collective-permute-start.1 = (f32[513,3,1,128]{3,2,1,0:T(1,128)S(1)}, f32[513,3,1,128]{3,2,1,0:T(1,128)S(1)}, u32[]{:S(2)}, u32[]{:S(2)}) collective-permute-start(f32[513,3,1,128]{3,2,1,0:T(1,128)S(1)} %get-tuple-element.90), channel_id=1, source_target_pairs={{1,0},{3,2},{5,4},{7,6},{9,8},{11,10},{13,12},{15,14},{17,16},{19,... | collective-permute-start | bytes 2363912 | tf_op jit(solution)/shard_map/ppermute | solution.py:18
  16.2 8.5 copy-start.19
  16.2 9.2 copy-start.26
  16.2 9.7 copy-start.21
  274.0 4.5 copy-start.1
  279.5 5.0 collective-permute-start.2
  282.7 4.2 collective-permute-start.3
  491.3 16.3 copy-start.16
  491.3 16.3 copy-start.24
  507.6 18.7 %copy-start.18 = (f32[1,3,3,9]{3,2,1,0:T(4,128)S(1)}, f32[1,3,3,9]{3,2,1,0:T(4,128)}, u32[]{:S(2)}) copy-start(f32[1,3,3,9]{3,2,1,0:T(4,128)} %get-tuple-element.119) | copy-start | bytes 976
  507.6 18.8 %copy-start.20 = (s32[512]{0:T(512)S(1)}, s32[512]{0:T(512)}, u32[]{:S(2)}) copy-start(s32[512]{0:T(512)} %param.14) | copy-start | bytes 6148
  507.6 18.8 %copy-start.22 = (f32[3]{0:T(128)S(1)}, f32[3]{0:T(128)}, u32[]{:S(2)}) copy-start(f32[3]{0:T(128)} %param.19) | copy-start | bytes 40
  517.3 4.5 copy-start
  522.9 4.2 collective-permute-start.4
  525.0 4.2 collective-permute-start.5
  733.6 16.3 copy-start.17
  733.6 16.3 copy-start.23
  766.3 4.1 copy-start.25
  770.3 204.5 %reduce-scatter.3.cloned.1.call-start = ((), (), s32[]{:S(2)}) async-start(), calls=%async_computation.3 | async-start | bytes 8912896 | tf_op jit(solution)/shard_map/reduce_scatter | solution.py:122
  794.7 216.2 %all-reduce.5.cloned.1.call-start = ((), (), s32[]{:S(2)}) async-start(), calls=%async_computation.4 | async-start | bytes 8388608 | tf_op jit(solution)/shard_map/psum | solution.py:140
  980.1 212.2 %reduce-scatter.5.cloned.1.call-start = ((), (), s32[]{:S(2)}) async-start(), calls=%async_computation.6 | async-start | bytes 8912896 | tf_op jit(solution)/shard_map/reduce_scatter | solution.py:142
  992.0 377.3 %all-reduce.7.cloned.1.call-start = ((), (), s32[]{:S(2)}) async-start(), calls=%async_computation.5 | async-start | bytes 8388608 | tf_op jit(solution)/shard_map/psum | solution.py:140
  1371.9 1.9 copy-start.2
  1521.1 1.0 copy-start.5
  1533.9 0.6 copy-start.14
  1585.2 0.7 copy-start.11
  1651.9 49.9 %copy-start.3 = (f32[512,512]{1,0:T(8,128)S(1)}, f32[512,512]{1,0:T(8,128)}, u32[]{:S(2)}) copy-start(f32[512,512]{1,0:T(8,128)} %get-tuple-element.254) | copy-start | bytes 3145732
  1695.5 1.6 copy-start.9
  1697.1 2.8 copy-start.12
  1699.9 1.2 copy-start.15
  1701.1 0.6 copy-start.8
  1704.2 8.2 copy-start.6
  1709.3 12.1 copy-start.4
  1717.8 5.8 copy-start.7
  1717.8 5.8 copy-start.10
  1717.8 5.8 copy-start.13
Sparse Core Ops, SparseCore 0:
  770.5 15.7 all-gather.1
  794.9 179.9 reduce-scatter.2
  980.2 30.7 all-reduce.4
  1013.2 178.9 reduce-scatter.4
  1198.7 170.5 all-reduce.6
